TPU v7x, 32 devices: a whole 2x2x4 slice. The times are simulated.
32 devices in a mesh: dp: 4 (over y, core), cells: 8 (over z, x).
Axes of the slice: x: 2, y: 2, z: 4, core: 2. Of those that a mesh axis runs over, the one named last changes fastest.
Arguments:
- sensitivity: float32 [8192, 12288], P('dp', 'cells'), may hold values from -0.0546875 to 0.0546875
- observed: float32 [8192, 256], P('dp'), may hold values from -6 to 6
- models: float32 [12288, 256], P('cells'), may hold values from -6 to 6
- neighbour_map: int32 [4, 768], replicated, may hold values from 0 to 767, as said below
- edge_mask: int32 [12288], P('cells'), may hold values 0 or 1
Outputs:
- updated: float32 [12288, 256], P('cells')
Inputs may be any that keep to these rules, and one draw needn't show every extreme that they name: `neighbour_map`: each row k maps every cell of a periodic 32 by 24 plane grid, numbered in a drawn order, to its neighbour in one of the four grid directions; every row is a permutation.
All inputs are finite; a program needn't handle non-finite values. No bound on the sum of `edge_mask` on one device may be relied on, other than what follows from the above.
Results may differ from a plain program's by a relative error of at most 0.0001.
Values sent between devices are 32-bit elements; how exact they have to be, the bound alone decides.
A program may use at most 128 MiB of HBM per device.

v0:
```python
import jax
import jax.numpy as jnp
from jax import lax
from jax.sharding import PartitionSpec as P

ITERS = 2


def with_halo(cells, sides, width):
    for axis, dim in sides:
        count = lax.axis_size(axis)
        ends = count - 1
        head = lax.slice_in_dim(cells, 0, width, axis=dim)
        tail = lax.slice_in_dim(cells, cells.shape[dim] - width, cells.shape[dim], axis=dim)
        cells = jnp.concatenate(
            [
                lax.ppermute(tail, axis, [(i, (i + 1) % count) for i in range(ends)]),
                cells,
                lax.ppermute(head, axis, [((i + 1) % count, i) for i in range(ends)]),
            ],
            axis=dim,
        )
    return cells


def reweight(misfit):
    return misfit / jnp.maximum(jnp.abs(misfit), 1.0)


def smooth_local(current, neighbour_map, edge_mask):
    plane_cells = neighbour_map.shape[1]
    count = current.shape[0] // plane_cells
    planes = current.reshape(count, plane_cells, current.shape[1])
    padded = with_halo(planes, (("cells", 0),), 1)
    total = jnp.zeros_like(planes)
    for other in (padded[:-2], padded[2:]):
        diff = other - planes
        total = total + diff / jnp.sqrt(1.0 + diff * diff)
    for k in range(4):
        other = jnp.take(planes, neighbour_map[k], axis=1)
        diff = other - planes
        total = total + diff / jnp.sqrt(1.0 + diff * diff)
    scale = 1.0 - 0.75 * edge_mask.astype(jnp.float32).reshape(count, plane_cells, 1)
    return (total * scale).reshape(current.shape)


def local(sensitivity, observed, models, neighbour_map, edge_mask):
    current = models
    for step in range(ITERS):
        predicted = lax.psum(
            jnp.dot(
                sensitivity,
                current,
                precision=lax.Precision.HIGHEST,
                preferred_element_type=jnp.float32,
            ),
            "cells",
        )
        weighted = reweight(predicted - observed)
        smooth = smooth_local(current, neighbour_map, edge_mask)
        partial_grad = lax.dot_general(
            sensitivity,
            weighted,
            (((0,), (0,)), ((), ())),
            precision=lax.Precision.HIGHEST,
            preferred_element_type=jnp.float32,
        )
        gradient = lax.psum(partial_grad, "dp")
        current = current - 1.0 * gradient + 0.05 * smooth
    return current


def solution(mesh):
    return jax.shard_map(
        local,
        mesh=mesh,
        in_specs=(P("dp", "cells"), P("dp", None), P("cells", None), P(), P("cells")),
        out_specs=P("cells", None),
        check_vma=False,
    )
```

profile of v0, /device:TPU:0, one launch (start us, length us, event | category | flops | bytes accessed | tf_op | source)
XLA Modules:
  0.0 418.7 jit_solution(4675436302633939359)
XLA Ops:
  6.5 0.0 all-reduce.5.cloned.1.call-start
  6.5 13.9 %fusion.16 = f32[2048,256]{1,0:T(8,128)} fusion(f32[2048,1536]{1,0:T(8,128)} %param.7, f32[1536,256]{1,0:T(8,128)} %param.9), kind=kOutput, calls=%fused_computation.72 | convolution fusion | flops 9663676416 | bytes 16252928 | tf_op jit(solution)/shard_map/dot_general | solution.py:51
  20.5 0.0 copy-start
  20.5 0.0 all-reduce.5.cloned.1.call-update
  20.5 0.0 copy-start.4
  20.5 0.0 all-reduce.7.cloned.1.call-start
  20.6 1.3 copy-done
  21.9 1.3 slice_bitcast_fusion.3
  23.1 5.7 %collective-permute-start = (f32[1,768,256]{2,1,0:T(8,128)}, f32[1,768,256]{2,1,0:T(8,128)}, u32[]{:S(2)}, u32[]{:S(2)}) collective-permute-start(f32[1,768,256]{2,1,0:T(8,128)} %get-tuple-element.12), channel_id=1, source_target_pairs={{0,1},{1,2},{2,3},{3,4},{4,5},{5,6},{6,7},{8,9},{9,10},{10,11},{11... | collective-permute-start | bytes 2359304 | tf_op jit(solution)/shard_map/ppermute | solution.py:17
  28.9 1.3 collective-permute-start.1
  30.2 0.0 copy-done.4
  30.2 0.0 copy-start.3
  30.2 1.2 copy.73
  31.4 0.0 copy-done.3
  31.5 4.0 gather_fusion.3
  35.5 4.0 gather_fusion.2
  39.6 4.0 gather_fusion.1
  43.6 4.1 gather_fusion
  47.7 96.1 %all-reduce.5.cloned.1.call-done = f32[2048,256]{1,0:T(8,128)} async-done(((f32[2048,256]{1,0:T(8,128)}), f32[2048,256]{1,0:T(8,128)}) %all-reduce.5.cloned.1.call-update) | async-done | bytes 2097168 | tf_op jit(solution)/shard_map/psum | solution.py:50
  143.8 25.0 %convolution_bitcast_fusion.2 = f32[1536,256]{1,0:T(8,128)} fusion(f32[2048,1536]{1,0:T(8,128)} %param.7, f32[2048,256]{1,0:T(8,128)} %all-reduce.5.cloned.1.call-done, f32[2048,256]{1,0:T(8,128)} %param.8), kind=kOutput, calls=%fused_computation.10 | convolution fusion | flops 9665773568 | bytes 18350080 | tf_op jit(solution)/shard_map/dot_general | solution.py:61
  168.8 0.0 copy-start.1
  168.8 0.0 all-reduce.7.cloned.1.call-update
  168.8 0.0 all-reduce.9.cloned.1.call-start
  168.9 0.0 collective-permute-done
  168.9 0.0 collective-permute-done.1
  168.9 1.3 copy-done.1
  170.2 6.2 %multiply_multiply_fusion.1 = f32[2,768,256]{2,1,0:T(8,128)} fusion(f32[2,768,256]{2,1,0:T(8,128)S(1)} %bitcast.61, f32[768,2,256]{2,1,0:T(2,128)S(1)} %copy-done.1, f32[768,2,256]{2,1,0:T(2,128)} %gather_fusion.2, f32[768,2,256]{2,1,0:T(2,128)} %gather_fusion.1, f32[768,2,256]{2,1,0:T(2,128)} %gather_fusion, f32[1,768,256]{2,1,0:T(8,128)} %collective-permute-done.1, ...), kind=kLoop, calls=%fused_computation.46 | loop fusion | flops 14548992 | bytes 11019264 | tf_op jit(solution)/shard_map/mul | solution.py:69
  176.4 34.7 %all-reduce.7.cloned.1.call-done = f32[1536,256]{1,0:T(8,128)} async-done(((f32[1536,256]{1,0:T(8,128)}), f32[1536,256]{1,0:T(8,128)}) %all-reduce.7.cloned.1.call-update) | async-done | bytes 1572880 | tf_op jit(solution)/shard_map/psum | solution.py:68
  211.1 2.2 bitcast_add_fusion.1
  213.3 13.5 %convolution_bitcast_fusion.1 = f32[2048,256]{1,0:T(8,128)} fusion(f32[1536,256]{1,0:T(8,128)S(1)} %bitcast_add_fusion.1, f32[2048,1536]{1,0:T(8,128)} %param.7), kind=kOutput, calls=%fused_computation.9 | convolution fusion | flops 9663676416 | bytes 16252928 | tf_op jit(solution)/shard_map/dot_general | solution.py:51
  226.8 0.0 all-reduce.9.cloned.1.call-update
  226.8 0.0 all-reduce.11.cloned.1.call-start
  226.9 1.2 copy.83
  228.1 4.0 gather_fusion.7
  232.1 4.0 gather_fusion.6
  236.1 4.0 gather_fusion.5
  240.2 4.1 gather_fusion.4
  244.2 1.3 slice_bitcast_fusion.1
  245.5 4.2 %collective-permute-start.2 = (f32[1,768,256]{2,1,0:T(8,128)}, f32[1,768,256]{2,1,0:T(8,128)}, u32[]{:S(2)}, u32[]{:S(2)}) collective-permute-start(f32[1,768,256]{2,1,0:T(8,128)} %get-tuple-element.10), channel_id=1, source_target_pairs={{0,1},{1,2},{2,3},{3,4},{4,5},{5,6},{6,7},{8,9},{9,10},{10,11},{11... | collective-permute-start | bytes 2359304 | tf_op jit(solution)/shard_map/ppermute | solution.py:17
  249.7 1.3 collective-permute-start.3
  251.0 90.5 %all-reduce.9.cloned.1.call-done = f32[2048,256]{1,0:T(8,128)} async-done(((f32[2048,256]{1,0:T(8,128)}), f32[2048,256]{1,0:T(8,128)}) %all-reduce.9.cloned.1.call-update) | async-done | bytes 2097168 | tf_op jit(solution)/shard_map/psum | solution.py:50
  341.5 24.8 %convolution_bitcast_fusion = f32[1536,256]{1,0:T(8,128)} fusion(f32[2048,1536]{1,0:T(8,128)} %param.7, f32[2048,256]{1,0:T(8,128)} %all-reduce.9.cloned.1.call-done, f32[2048,256]{1,0:T(8,128)} %param.8), kind=kOutput, calls=%fused_computation.8 | convolution fusion | flops 9665773568 | bytes 18350080 | tf_op jit(solution)/shard_map/dot_general | solution.py:61
  366.3 0.0 copy-start.2
  366.3 0.0 all-reduce.11.cloned.1.call-update
  366.3 0.0 collective-permute-done.2
  366.3 0.0 collective-permute-done.3
  366.3 1.4 copy-done.2
  367.7 6.1 %multiply_multiply_fusion = f32[2,768,256]{2,1,0:T(8,128)} fusion(f32[2,768,256]{2,1,0:T(8,128)S(1)} %bitcast.59, f32[768,2,256]{2,1,0:T(2,128)S(1)} %copy-done.2, f32[768,2,256]{2,1,0:T(2,128)} %gather_fusion.6, f32[768,2,256]{2,1,0:T(2,128)} %gather_fusion.5, f32[768,2,256]{2,1,0:T(2,128)} %gather_fusion.4, f32[1,768,256]{2,1,0:T(8,128)} %collective-permute-done.3, ...), kind=kLoop, calls=%fused_computation.45 | loop fusion | flops 14548992 | bytes 11019264 | tf_op jit(solution)/shard_map/mul | solution.py:69
  373.8 34.8 %all-reduce.11.cloned.1.call-done = f32[1536,256]{1,0:T(8,128)} async-done(((f32[1536,256]{1,0:T(8,128)}), f32[1536,256]{1,0:T(8,128)}) %all-reduce.11.cloned.1.call-update) | async-done | bytes 1572880 | tf_op jit(solution)/shard_map/psum | solution.py:68
  408.6 3.3 bitcast_add_fusion
  (11 shorter events, 0.1 us)
Async XLA Ops:
  6.5 137.2 %all-reduce.5.cloned.1.call-start = ((), (), s32[]{:S(2)}) async-start(), calls=%async_computation | async-start | bytes 4194304 | tf_op jit(solution)/shard_map/psum | solution.py:50
  20.5 1.4 copy-start
  20.5 9.7 %copy-start.4 = (s32[1536]{0:T(1024)S(1)}, s32[1536]{0:T(1024)}, u32[]{:S(2)}) copy-start(s32[1536]{0:T(1024)} %param.11) | copy-start | bytes 18436
  20.5 190.6 %all-reduce.7.cloned.1.call-start = ((), (), s32[]{:S(2)}) async-start(), calls=%async_computation.1 | async-start | bytes 3145728 | tf_op jit(solution)/shard_map/psum | solution.py:68
  23.1 145.7 %collective-permute-start = (f32[1,768,256]{2,1,0:T(8,128)}, f32[1,768,256]{2,1,0:T(8,128)}, u32[]{:S(2)}, u32[]{:S(2)}) collective-permute-start(f32[1,768,256]{2,1,0:T(8,128)} %get-tuple-element.12), channel_id=1, source_target_pairs={{0,1},{1,2},{2,3},{3,4},{4,5},{5,6},{6,7},{8,9},{9,10},{10,11},{11... | collective-permute-start | bytes 2359304 | tf_op jit(solution)/shard_map/ppermute | solution.py:17
  28.9 140.0 %collective-permute-start.1 = (f32[1,768,256]{2,1,0:T(8,128)}, f32[1,768,256]{2,1,0:T(8,128)}, u32[]{:S(2)}, u32[]{:S(2)}) collective-permute-start(f32[1,768,256]{2,1,0:T(8,128)} %get-tuple-element.13), channel_id=1, source_target_pairs={{1,0},{2,1},{3,2},{4,3},{5,4},{6,5},{7,6},{9,8},{10,9},{11,10},{12... | collective-permute-start | bytes 2359304 | tf_op jit(solution)/shard_map/ppermute | solution.py:19
  30.2 1.2 copy-start.3
  168.8 1.4 copy-start.1
  168.8 172.7 %all-reduce.9.cloned.1.call-start = ((), (), s32[]{:S(2)}) async-start(), calls=%async_computation.2 | async-start | bytes 4194304 | tf_op jit(solution)/shard_map/psum | solution.py:50
  226.8 181.8 %all-reduce.11.cloned.1.call-start = ((), (), s32[]{:S(2)}) async-start(), calls=%async_computation.3 | async-start | bytes 3145728 | tf_op jit(solution)/shard_map/psum | solution.py:68
  245.5 120.8 %collective-permute-start.2 = (f32[1,768,256]{2,1,0:T(8,128)}, f32[1,768,256]{2,1,0:T(8,128)}, u32[]{:S(2)}, u32[]{:S(2)}) collective-permute-start(f32[1,768,256]{2,1,0:T(8,128)} %get-tuple-element.10), channel_id=1, source_target_pairs={{0,1},{1,2},{2,3},{3,4},{4,5},{5,6},{6,7},{8,9},{9,10},{10,11},{11... | collective-permute-start | bytes 2359304 | tf_op jit(solution)/shard_map/ppermute | solution.py:17
  249.7 116.6 %collective-permute-start.3 = (f32[1,768,256]{2,1,0:T(8,128)}, f32[1,768,256]{2,1,0:T(8,128)}, u32[]{:S(2)}, u32[]{:S(2)}) collective-permute-start(f32[1,768,256]{2,1,0:T(8,128)} %get-tuple-element.11), channel_id=1, source_target_pairs={{1,0},{2,1},{3,2},{4,3},{5,4},{6,5},{7,6},{9,8},{10,9},{11,10},{12... | collective-permute-start | bytes 2359304 | tf_op jit(solution)/shard_map/ppermute | solution.py:19
  366.3 1.4 copy-start.2
Sparse Core Ops, SparseCore 0:
  20.6 123.1 all-reduce.4
  168.9 42.1 all-reduce.6
  227.0 114.5 all-reduce.8
  366.4 42.1 all-reduce.10
where the time goes:
time: 426 us; the launch traced here: 419 us
  waiting for transfers between devices  256 us (60%)
  matrix products  77.2 us (18%)
  local copies, waits for them, and re-layouts  41.2 us (10%)
  other arithmetic  17.9 us (4%)
  between operations  13.5 us (3%)
  starting transfers between devices  12.7 us (3%)
    psum x2, waiting for transfers between devices, local(): lax.psum(jnp.dot(sensitivity, current, precision=lax.Precision.HIGHEST, p...  187 us
    psum x2, waiting for transfers between devices, local(): gradient = lax.psum(partial_grad, 'dp')  69.5 us
    dot_general x2, matrix products, local(): lax.dot_general(sensitivity, weighted, (((0,), (0,)), ((), ())), precisio...  49.8 us
    gather x8, local copies, waits for them, and re-layouts, smooth_local(): other = jnp.take(planes, neighbour_map[k], axis=1)  32.2 us
    dot_general x2, matrix products, local(): jnp.dot(sensitivity, current, precision=lax.Precision.HIGHEST, preferred_...  27.5 us
    mul x2, other arithmetic, local(): current = current - 1.0 * gradient + 0.05 * smooth  12.3 us
    ppermute x2, starting transfers between devices, with_halo(): lax.ppermute(tail, axis, [(i, (i + 1) % count) for i in range(ends)])  9.98 us
  transfers between devices with their start and end apart: 8, of which 4 were waited for; matrix products, arithmetic and copies ran while one was open for 24% of the time, Pallas kernels for 0%

commit v1 on v0

--- a/solution.py
+++ b/solution.py
@@ -47,14 +47,17 @@
 def local(sensitivity, observed, models, neighbour_map, edge_mask):
     current = models
     for step in range(ITERS):
-        predicted = lax.psum(
-            jnp.dot(
-                sensitivity,
-                current,
-                precision=lax.Precision.HIGHEST,
-                preferred_element_type=jnp.float32,
+        predicted = jnp.sum(
+            lax.all_gather(
+                jnp.dot(
+                    sensitivity,
+                    current,
+                    precision=lax.Precision.HIGHEST,
+                    preferred_element_type=jnp.float32,
+                ),
+                "cells",
             ),
-            "cells",
+            axis=0,
         )
         weighted = reweight(predicted - observed)
         smooth = smooth_local(current, neighbour_map, edge_mask)

time: 426 us -> 720 us (1.69)
  waiting for transfers between devices: 256 us -> 503 us
  local copies, waits for them, and re-layouts: 41.2 us -> 61.7 us
  other arithmetic: 17.9 us -> 32.7 us
  matrix products: 77.2 us -> 87.4 us
    all_gather x0 -> x2, waiting for transfers between devices: none -> 435 us  [local(): lax.all_gather(jnp.dot(sensitivity, current, precision=lax.Precision.HIGH...]
    psum x2 -> x0, waiting for transfers between devices: 187 us -> none  [local(): lax.psum(jnp.dot(sensitivity, current, precision=lax.Precision.HIGHEST, p...]
    unnamed x10 -> x11, local copies, waits for them, and re-layouts: 4.01 us -> 21.6 us
    reduce_sum x0 -> x2, other arithmetic: none -> 15.2 us  [local(): jnp.sum(lax.all_gather(jnp.dot(sensitivity, current, precision=lax.Precis...]
    dot_general x2, matrix products: 27.5 us -> 38 us  [local(): jnp.dot(sensitivity, current, precision=lax.Precision.HIGHEST, preferred_...]
  transfers between devices with their start and end apart: 8 -> 8, of which waited for: 4 -> 4; matrix products, arithmetic and copies ran while one was open for 24% -> 19% of each run, Pallas kernels for 0% -> 0%
where the time goes in v1:
time: 720 us; the launch traced here: 712 us
  waiting for transfers between devices  503 us (70%)
  matrix products  87.4 us (12%)
  local copies, waits for them, and re-layouts  61.7 us (9%)
  other arithmetic  32.7 us (5%)
  between operations  13.5 us (2%)
  starting transfers between devices  13.2 us (2%)
    all_gather x2, waiting for transfers between devices, local(): lax.all_gather(jnp.dot(sensitivity, current, precision=lax.Precision.HIGH...  435 us
    psum x2, waiting for transfers between devices, local(): gradient = lax.psum(partial_grad, 'dp')  67.6 us
    dot_general x2, matrix products, local(): lax.dot_general(sensitivity, weighted, (((0,), (0,)), ((), ())), precisio...  49.5 us
    dot_general x2, matrix products, local(): jnp.dot(sensitivity, current, precision=lax.Precision.HIGHEST, preferred_...  38 us
    gather x8, local copies, waits for them, and re-layouts, smooth_local(): other = jnp.take(planes, neighbour_map[k], axis=1)  32.1 us
    unnamed x11, local copies, waits for them, and re-layouts  21.6 us
    reduce_sum x2, other arithmetic, local(): jnp.sum(lax.all_gather(jnp.dot(sensitivity, current, precision=lax.Precis...  15.2 us
  transfers between devices with their start and end apart: 8, of which 4 were waited for; matrix products, arithmetic and copies ran while one was open for 19% of the time, Pallas kernels for 0%

profile of v1, /device:TPU:0, one launch (start us, length us, event | category | flops | bytes accessed | tf_op | source)
XLA Modules:
  0.0 711.7 jit_solution(16524376959208173480)
XLA Ops:
  6.5 0.0 all-gather.5.cloned.1.call-start
  6.5 13.9 %fusion.16 = f32[2048,256]{1,0:T(8,128)} fusion(f32[2048,1536]{1,0:T(8,128)} %param.7, f32[1536,256]{1,0:T(8,128)} %param.9), kind=kOutput, calls=%fused_computation.73 | convolution fusion | flops 9663676416 | bytes 16252928 | tf_op jit(solution)/shard_map/dot_general | solution.py:52
  20.5 0.0 copy-start
  20.5 0.0 all-gather.5.cloned.1.call-update
  20.5 0.0 all-reduce.3.cloned.1.call-start
  20.6 1.3 copy-done
  21.9 1.3 slice_bitcast_fusion.3
  23.2 5.8 collective-permute-start
  29.0 1.3 collective-permute-start.1
  30.3 0.0 copy-start.3
  30.3 1.2 copy.135
  31.5 0.0 copy-done.3
  31.6 4.0 gather_fusion.2
  35.6 4.0 gather_fusion
  39.7 4.0 gather_fusion.1
  43.7 0.0 copy-start.4
  43.7 4.0 gather_fusion.3
  47.7 0.0 copy-done.4
  47.7 216.2 %all-gather.5.cloned.1.call-done = f32[16384,256]{1,0:T(8,128)} async-done(((f32[2048,256]{1,0:T(8,128)}), f32[16384,256]{1,0:T(8,128)}) %all-gather.5.cloned.1.call-update) | async-done | bytes 16777232 | tf_op jit(solution)/shard_map/all_gather | solution.py:51
  263.9 8.5 %reduce_sum.18 = f32[2048,256]{1,0:T(8,128)} reduce(f32[8,2048,256]{2,1,0:T(8,128)} %bitcast.68, f32[]{:T(128)} %constant.0.clone.1), dimensions={0}, to_apply=%region_0.0 | reduce | flops 3670016 | bytes 18874372 | tf_op jit(solution)/shard_map/reduce_sum | solution.py:50
  272.4 24.7 %convolution_bitcast_fusion.2 = f32[1536,256]{1,0:T(8,128)} fusion(f32[2048,1536]{1,0:T(8,128)} %param.7, f32[2048,256]{1,0:T(8,128)} %reduce_sum.18, f32[2048,256]{1,0:T(8,128)} %param.8), kind=kOutput, calls=%fused_computation.11 | convolution fusion | flops 9665773568 | bytes 18350080 | tf_op jit(solution)/shard_map/dot_general | solution.py:64
  297.1 0.0 copy-start.1
  297.1 0.0 all-reduce.3.cloned.1.call-update
  297.1 0.0 all-gather.7.cloned.1.call-start
  297.2 0.0 collective-permute-done
  297.2 0.0 collective-permute-done.1
  297.2 1.3 copy-done.1
  298.5 6.0 multiply_multiply_fusion.1
  304.6 33.8 %all-reduce.3.cloned.1.call-done = f32[1536,256]{1,0:T(8,128)} async-done(((f32[1536,256]{1,0:T(8,128)}), f32[1536,256]{1,0:T(8,128)}) %all-reduce.3.cloned.1.call-update) | async-done | bytes 1572880 | tf_op jit(solution)/shard_map/psum | solution.py:71
  338.3 2.2 bitcast_add_fusion.1
  340.5 24.0 %convolution_bitcast_fusion.1 = f32[2048,256]{0,1:T(8,128)} fusion(f32[1536,256]{1,0:T(8,128)S(1)} %bitcast_add_fusion.1, f32[2048,1536]{1,0:T(8,128)} %param.7), kind=kOutput, calls=%fused_computation.10 | convolution fusion | flops 9663676416 | bytes 16252928 | tf_op jit(solution)/shard_map/dot_general | solution.py:52
  364.5 0.0 all-gather.7.cloned.1.call-update
  364.6 0.4 all-reduce.5.cloned.1.call-start
  365.0 1.2 copy.145
  366.2 4.0 gather_fusion.4
  370.3 4.0 gather_fusion.5
  374.3 4.0 gather_fusion.6
  378.3 4.0 gather_fusion.7
  382.3 1.3 slice_bitcast_fusion.1
  383.6 4.3 collective-permute-start.2
  387.9 1.3 collective-permute-start.3
  389.2 219.3 %all-gather.7.cloned.1.call-done = f32[16384,256]{0,1:T(8,128)} async-done(((f32[2048,256]{0,1:T(8,128)}), f32[16384,256]{0,1:T(8,128)}) %all-gather.7.cloned.1.call-update) | async-done | bytes 16777232 | tf_op jit(solution)/shard_map/all_gather | solution.py:51
  608.5 17.6 %copy.155 = f32[32,8,8,2048]{3,2,1,0:T(8,128)S(1)} copy(f32[32,8,8,2048]{3,1,2,0:T(8,128)} %bitcast.69) | data formatting | bytes 33554432
  626.1 6.7 bitcast_reduce_fusion
  632.8 2.9 copy.143
  635.7 24.7 %convolution_bitcast_fusion = f32[1536,256]{1,0:T(8,128)} fusion(f32[2048,1536]{1,0:T(8,128)} %param.7, f32[2048,256]{1,0:T(8,128)} %copy.143, f32[2048,256]{1,0:T(8,128)} %param.8), kind=kOutput, calls=%fused_computation.9 | convolution fusion | flops 9665773568 | bytes 18350080 | tf_op jit(solution)/shard_map/dot_general | solution.py:64
  660.4 0.0 copy-start.2
  660.4 0.0 all-reduce.5.cloned.1.call-update
  660.4 0.0 collective-permute-done.2
  660.5 0.0 collective-permute-done.3
  660.5 1.4 copy-done.2
  661.8 6.0 multiply_multiply_fusion
  667.8 33.8 %all-reduce.5.cloned.1.call-done = f32[1536,256]{1,0:T(8,128)} async-done(((f32[1536,256]{1,0:T(8,128)}), f32[1536,256]{1,0:T(8,128)}) %all-reduce.5.cloned.1.call-update) | async-done | bytes 1572880 | tf_op jit(solution)/shard_map/psum | solution.py:71
  701.6 3.3 bitcast_add_fusion
  (11 shorter events, 0.1 us)
Async XLA Ops:
  6.5 257.4 %all-gather.5.cloned.1.call-start = ((), (), s32[]{:S(2)}) async-start(), calls=%async_computation.2 | async-start | bytes 18874368 | tf_op jit(solution)/shard_map/all_gather | solution.py:51
  20.5 1.4 copy-start
  20.5 317.8 %all-reduce.3.cloned.1.call-start = ((), (), s32[]{:S(2)}) async-start(), calls=%async_computation | async-start | bytes 3145728 | tf_op jit(solution)/shard_map/psum | solution.py:71
  23.2 274.0 %collective-permute-start = (f32[1,768,256]{2,1,0:T(8,128)}, f32[1,768,256]{2,1,0:T(8,128)}, u32[]{:S(2)}, u32[]{:S(2)}) collective-permute-start(f32[1,768,256]{2,1,0:T(8,128)} %get-tuple-element.12), channel_id=1, source_target_pairs={{0,1},{1,2},{2,3},{3,4},{4,5},{5,6},{6,7},{8,9},{9,10},{10,11},{11... | collective-permute-start | bytes 2359304 | tf_op jit(solution)/shard_map/ppermute | solution.py:17
  29.0 268.2 %collective-permute-start.1 = (f32[1,768,256]{2,1,0:T(8,128)}, f32[1,768,256]{2,1,0:T(8,128)}, u32[]{:S(2)}, u32[]{:S(2)}) collective-permute-start(f32[1,768,256]{2,1,0:T(8,128)} %get-tuple-element.13), channel_id=1, source_target_pairs={{1,0},{2,1},{3,2},{4,3},{5,4},{6,5},{7,6},{9,8},{10,9},{11,10},{12... | collective-permute-start | bytes 2359304 | tf_op jit(solution)/shard_map/ppermute | solution.py:19
  30.3 1.2 copy-start.3
  43.7 4.0 copy-start.4
  297.1 1.4 copy-start.1
  297.1 311.4 %all-gather.7.cloned.1.call-start = ((), (), s32[]{:S(2)}) async-start(), calls=%async_computation.3 | async-start | bytes 18874368 | tf_op jit(solution)/shard_map/all_gather | solution.py:51
  364.6 337.1 %all-reduce.5.cloned.1.call-start = ((), (), s32[]{:S(2)}) async-start(), calls=%async_computation.1 | async-start | bytes 3145728 | tf_op jit(solution)/shard_map/psum | solution.py:71
  383.6 276.8 %collective-permute-start.2 = (f32[1,768,256]{2,1,0:T(8,128)}, f32[1,768,256]{2,1,0:T(8,128)}, u32[]{:S(2)}, u32[]{:S(2)}) collective-permute-start(f32[1,768,256]{2,1,0:T(8,128)} %get-tuple-element.10), channel_id=1, source_target_pairs={{0,1},{1,2},{2,3},{3,4},{4,5},{5,6},{6,7},{8,9},{9,10},{10,11},{11... | collective-permute-start | bytes 2359304 | tf_op jit(solution)/shard_map/ppermute | solution.py:17
  387.9 272.6 %collective-permute-start.3 = (f32[1,768,256]{2,1,0:T(8,128)}, f32[1,768,256]{2,1,0:T(8,128)}, u32[]{:S(2)}, u32[]{:S(2)}) collective-permute-start(f32[1,768,256]{2,1,0:T(8,128)} %get-tuple-element.11), channel_id=1, source_target_pairs={{1,0},{2,1},{3,2},{4,3},{5,4},{6,5},{7,6},{9,8},{10,9},{11,10},{12... | collective-permute-start | bytes 2359304 | tf_op jit(solution)/shard_map/ppermute | solution.py:19
  660.4 1.4 copy-start.2
Sparse Core Ops, SparseCore 0:
  20.6 243.2 all-gather.4
  297.3 41.0 all-reduce.2
  364.7 243.7 all-gather.6
  660.6 41.0 all-reduce.4
